TPU v7x, 32 devices: a whole 2x2x4 slice. The times are simulated.
32 devices in a mesh: seq: 8 (over z, y), head: 4 (over x, core).
Axes of the slice: x: 2, y: 2, z: 4, core: 2. Of those that a mesh axis runs over, the one named last changes fastest.
Arguments:
- queries: bfloat16 [4096, 1024], P('seq', 'head'), may hold values from -6 to 6
- keys: bfloat16 [4096, 1024], P('seq', 'head'), may hold values from -6 to 6
- values: bfloat16 [4096, 1024], P('seq', 'head'), may hold values from -4 to 4
- masked: int32 [4096], P('seq'), may hold values from 0 to 1
- mask_qkv: bfloat16 [3, 1024], P(None, 'head'), may hold values from -5.09375 to 5.09375
- key_bars: int32 [32, 4], P('seq'), may hold values from -1 to 31, as said below
- w_out: bfloat16 [1024, 1536], P('head'), may hold values from -0.1875 to 0.1875
Outputs:
- attn_out: bfloat16 [4096, 1536], P('seq', 'head')
Inputs may be any that keep to these rules, and one draw needn't show every extreme that they name: `key_bars`: entry [b, s] is -1 or a bar on the device s - 2 places along seq for s < 2, s - 1 places for s >= 2. Bar b lists bar a in slot s exactly when a lists b in slot 3 - s. No listed bar is b or next to b. The bars of one device list at most 2 bars of any one other device, and some pair of devices reaches 2.
All inputs are finite; a program needn't handle non-finite values.
Results may differ from a plain program's by a relative error of at most 0.009.
Values may be sent and summed in bfloat16 or wider, within the bound.
A program may use at most 64 MiB of HBM per device.

v0:
```python
import functools

import jax
import jax.numpy as jnp
from jax import lax
from jax.experimental import pallas as pl
from jax.experimental.pallas import tpu as pltpu
from jax.sharding import PartitionSpec as P

HD = 64
R = 2
CAP = 2
CHUNK = 1
LANES = 128
MESH = pl.DeviceIdType.MESH
NEG = -1e30


def kernel(
    n_seq, n_head, bars_hbm, masked_hbm, mask_hbm, q_hbm, k_hbm, v_hbm, w_ref, out_ref,
    bars_ref, masked_ref, mask_ref, small_sem, q_ref, k_ref, v_ref, in_sem,    kv, qs, pack, got_refs, rim, w_all, att, top, tot, acc,
    halo_send, halo_recv, rim_send, rim_recv, w_send, w_recv, w_own, att_send, att_recv,
):
    seq = lax.axis_index("seq")
    head = lax.axis_index("head")
    bar_count, bar_len, width = q_ref.shape
    tiles = width // LANES
    per_tile = LANES // HD
    out_cols = w_all.shape[2]
    columns = 2 * R
    got = [got_refs[c * tiles : (c + 1) * tiles] for c in range(columns)]
    offsets = [c - R if c < R else c - R + 1 for c in range(columns)]
    low, high = R - 1, R

    def there(offset):
        return jnp.logical_and(seq + offset >= 0, seq + offset < n_seq)

    barrier = pltpu.get_barrier_semaphore()
    count = n_head - 1
    for offset in offsets:
        count = count + there(offset).astype(jnp.int32)

        @pl.when(there(offset))
        def _(offset=offset):
            pl.semaphore_signal(
                barrier, inc=1, device_id=(seq + offset, head), device_id_type=MESH
            )

    peers = [lax.rem(head + step, n_head) for step in range(1, n_head)]
    for peer in peers:
        pl.semaphore_signal(barrier, inc=1, device_id=(seq, peer), device_id_type=MESH)

    small = [
        pltpu.make_async_copy(source, target, small_sem.at[n])
        for n, (source, target) in enumerate(
            ((masked_hbm, masked_ref), (mask_hbm, mask_ref), (bars_hbm, bars_ref))
        )
    ]
    for load in small:
        load.start()
    bar_order = [bar_count - 1, 0] + list(range(1, bar_count - 1))
    loads = {}
    for n, (source, target) in enumerate(((k_hbm, k_ref), (v_hbm, v_ref))):
        for b in range(bar_count):
            loads[n, b] = pltpu.make_async_copy(source.at[b], target.at[b], in_sem.at[n, b])
    for b in bar_order:
        loads[0, b].start()
        loads[1, b].start()
    q_load = pltpu.make_async_copy(q_hbm, q_ref, in_sem.at[2, 0])
    q_load.start()
    own_w = pltpu.make_async_copy(
        w_ref.at[:, pl.ds(pl.multiple_of(head * out_cols, LANES), out_cols)],
        w_all.at[head],
        w_own,
    )
    own_w.start()

    rows = lax.broadcasted_iota(jnp.int32, (bar_len, bar_len), 0)
    cols = lax.broadcasted_iota(jnp.int32, (bar_len, bar_len), 1)

    def flag(b):
        row = masked_ref[b : b + 1, :]
        return jnp.max(jnp.where(rows == cols, row, 0), axis=1, keepdims=True) == 1

    def replaced(value, row, hit):
        return jnp.where(hit, mask_ref[row : row + 1, :].astype(jnp.float32), value.astype(jnp.float32))

    def prepare(b):
        loads[0, b].wait()
        loads[1, b].wait()
        hit = flag(b)
        key_eff = replaced(k_ref[b], 1, hit).astype(jnp.bfloat16)
        value_eff = replaced(v_ref[b], 2, hit).astype(jnp.bfloat16)
        for t in range(tiles):
            kv[t, b, :, :LANES] = key_eff[:, t * LANES : (t + 1) * LANES]
            kv[t, b, :, LANES:] = value_eff[:, t * LANES : (t + 1) * LANES]

    for load in small:
        load.wait()
    for b in bar_order[:2]:
        prepare(b)

    listed = [[bars_ref[b, c] for c in range(columns)] for b in range(bar_count)]
    picks = []
    for c in range(columns):
        before = jnp.int32(0)
        chosen = [jnp.int32(0)] * CAP
        for b in range(bar_count):
            used = (listed[b][c] >= 0).astype(jnp.int32)
            for slot in range(CAP):
                chosen[slot] = chosen[slot] + jnp.where(before == slot, used * b, 0)
            before = before + used
        picks.append(chosen)

    pl.semaphore_wait(barrier, count)

    def halo(c, t):
        return pltpu.make_async_remote_copy(
            src_ref=pack.at[c, t],
            dst_ref=got[columns - 1 - c][t],
            send_sem=halo_send.at[c, t],
            recv_sem=halo_recv.at[columns - 1 - c, t],
            device_id=(seq + offsets[c], head),
            device_id_type=MESH,
        )

    def edge(side, t):
        return pltpu.make_async_remote_copy(
            src_ref=kv.at[t, bar_count - 1 if side else 0],
            dst_ref=rim.at[1 - side, t],
            send_sem=rim_send.at[side, t],
            recv_sem=rim_recv.at[1 - side, t],
            device_id=(seq + (1 if side else -1), head),
            device_id_type=MESH,
        )

    far = [c for c in range(columns) if c not in (low, high)]
    for c in (low, high):

        @pl.when(there(offsets[c]))
        def _(c=c):
            edge(c - low, 0).start()

    for b in bar_order[2:]:
        prepare(b)
    stages = [(t, c) for group in (far, (low, high)) for t in range(tiles) for c in group]
    for t, c in stages:
        for slot in range(CAP):
            pack[c, t, slot] = kv[t, picks[c][slot]]

        @pl.when(there(offsets[c]))
        def _(c=c, t=t):
            if c in (low, high) and t > 0:
                edge(c - low, t).start()
            halo(c, t).start()

        @pl.when(jnp.logical_not(there(offsets[c])))
        def _(c=c, t=t):
            got[c][t][...] = jnp.zeros(got[c][t].shape, got[c][t].dtype)
            if c in (low, high):
                rim[c - low, t] = jnp.zeros(rim.shape[2:], rim.dtype)

    def w_copy(step):
        peer = peers[step]
        return pltpu.make_async_remote_copy(
            src_ref=w_ref.at[:, pl.ds(pl.multiple_of(peer * out_cols, LANES), out_cols)],
            dst_ref=w_all.at[head],
            send_sem=w_send.at[step],
            recv_sem=w_recv.at[step],
            device_id=(seq, peer),
            device_id_type=MESH,
        )

    for step in range(n_head - 1):
        w_copy(step).start()

    lane = lax.broadcasted_iota(jnp.int32, (bar_len, LANES), 1)
    scaling = HD ** -0.5
    q_load.wait()
    for b in range(bar_count):
        query = replaced(q_ref[b], 0, flag(b)) * scaling
        for t in range(tiles):
            part = query[:, t * LANES : (t + 1) * LANES]
            for h in range(per_tile):
                qs[b, t, h * bar_len : (h + 1) * bar_len, :] = jnp.where(
                    lane // HD == h, part, 0.0
                ).astype(jnp.bfloat16)

    def update(b, t, blocks, first=False, last=False):
        k_at, v_at = slice(0, LANES), slice(LANES, 2 * LANES)
        query = qs[b, t]
        scores = []
        for ref, index, usable in blocks:
            s = lax.dot_general(
                query, ref[index + (slice(None), k_at)], (((1,), (1,)), ((), ())),
                preferred_element_type=jnp.float32,
            )
            if usable is not None:
                s = s + jnp.where(usable, 0.0, NEG).astype(jnp.float32)
            scores.append(s)
        wide = functools.reduce(jnp.maximum, scores)
        peak = jnp.max(wide, axis=1, keepdims=True)
        if not first:
            old = top[b, t][:, :1]
            peak = jnp.maximum(peak, old)
            fade = jnp.exp(old - peak)
        raised = [jnp.exp(s - peak) for s in scores]
        total = jnp.sum(functools.reduce(jnp.add, raised), axis=1, keepdims=True)
        rounded = jnp.concatenate([r.astype(jnp.bfloat16) for r in raised], axis=1)
        value = jnp.concatenate([ref[index + (slice(None), v_at)] for ref, index, _ in blocks], axis=0)
        weighted = jnp.dot(rounded, value, preferred_element_type=jnp.float32)
        if not first:
            total = total + tot[b, t][:, :1] * fade
            weighted = weighted + acc[b, t] * fade
        if not last:
            top[b, t] = jnp.broadcast_to(peak, top.shape[2:])
            tot[b, t] = jnp.broadcast_to(total, tot.shape[2:])
            acc[b, t] = weighted
            return None
        done = weighted / total
        result = done[:bar_len]
        for h in range(1, per_tile):
            result = jnp.where(lane // HD == h, done[h * bar_len : (h + 1) * bar_len], result)
        return result.astype(jnp.bfloat16)

    for t in range(tiles):
        for b in range(bar_count):
            blocks = [(kv, (t, n), None) for n in range(max(b - 1, 0), min(b + 2, bar_count))]
            update(b, t, blocks, first=True)

    def listed_block(b, c, t):
        wanted = listed[b][c]
        slot = jnp.int32(0)
        for other in range(bar_count):
            held = listed[other][c]
            slot = slot + jnp.logical_and(held >= 0, held < wanted).astype(jnp.int32)
        return (got[c][t], (jnp.minimum(slot, CAP - 1),), wanted >= 0)

    twin = head + 1 - 2 * lax.rem(head, 2)
    across = lax.rem(head + 2, n_head)
    chunks = bar_count // CHUNK

    def att_copy(t, g, kind):
        slot = across if kind == 2 else head
        part = att.at[slot, t, g * CHUNK : (g + 1) * CHUNK]
        return pltpu.make_async_remote_copy(
            src_ref=part,
            dst_ref=part,
            send_sem=att_send.at[t, g, kind],
            recv_sem=att_recv.at[t, g, kind],
            device_id=(seq, across if kind == 1 else twin),
            device_id_type=MESH,
        )

    def relay(t, g):
        att_copy(t, g, 1).wait_recv()
        att_copy(t, g, 2).start()

    for t in range(tiles):
        for c in far:

            @pl.when(there(offsets[c]))
            def _(c=c, t=t):
                halo(columns - 1 - c, t).wait_recv()

        for b in range(bar_count):
            update(b, t, [listed_block(b, c, t) for c in far])
        if t > 0:
            for g in range(chunks):
                relay(t - 1, g)
        for c in (low, high):

            @pl.when(there(offsets[c]))
            def _(c=c, t=t):
                halo(columns - 1 - c, t).wait_recv()
                edge(high - c, t).wait_recv()

        for g in range(chunks):
            for b in range(g * CHUNK, (g + 1) * CHUNK):
                blocks = [listed_block(b, c, t) for c in (low, high)]
                if b == 0:
                    blocks.append((rim, (0, t), there(-1)))
                if b == bar_count - 1:
                    blocks.append((rim, (1, t), there(1)))
                att[head, t, b] = update(b, t, blocks, last=True)
            att_copy(t, g, 1).start()
            att_copy(t, g, 0).start()

    own_w.wait()
    for step in range(n_head - 1):
        w_copy(step).wait_recv()
    for g in range(chunks):
        relay(tiles - 1, g)
    for g in range(chunks):
        for t in range(tiles):
            att_copy(t, g, 0).wait_recv()
            att_copy(t, g, 2).wait_recv()
        for b in range(g * CHUNK, (g + 1) * CHUNK):
            summed = None
            for member in range(n_head):
                lhs = jnp.concatenate([att[member, t, b] for t in range(tiles)], axis=1)
                term = jnp.dot(lhs, w_all[member], preferred_element_type=jnp.float32)
                term = term.astype(jnp.bfloat16).astype(jnp.float32)
                summed = term if summed is None else summed + term
            out_ref[b] = summed.astype(jnp.bfloat16)

    for t in range(tiles):
        for c in range(columns):

            @pl.when(there(offsets[c]))
            def _(c=c, t=t):
                halo(c, t).wait_send()
                if c in (low, high):
                    edge(c - low, t).wait_send()

        for g in range(chunks):
            for kind in range(3):
                att_copy(t, g, kind).wait_send()
    for step in range(n_head - 1):
        w_copy(step).wait_send()


def solution(mesh):
    n_seq, n_head = mesh.shape["seq"], mesh.shape["head"]

    def on_device(queries, keys, values, masked, mask_qkv, key_bars, w_out):
        tokens, width = queries.shape
        bars = key_bars.shape[0]
        length = tokens // bars
        cols = w_out.shape[1] // n_head
        tiles, rows = width // LANES, LANES // HD * length
        shaped = [x.reshape(bars, length, width) for x in (queries, keys, values)]
        vmem = pl.BlockSpec(memory_space=pltpu.VMEM)
        dma = pltpu.SemaphoreType.DMA
        out = pl.pallas_call(
            functools.partial(kernel, n_seq, n_head),
            out_shape=jax.ShapeDtypeStruct((bars, length, cols), jnp.bfloat16),
            in_specs=[pl.BlockSpec(memory_space=pl.ANY)] * 7,
            out_specs=vmem,
            scratch_shapes=[
                pltpu.SMEM(key_bars.shape, jnp.int32),
                pltpu.VMEM((bars, length), jnp.int32),
                pltpu.VMEM(mask_qkv.shape, jnp.bfloat16),
                dma((3,)),
            ]
            + [pltpu.VMEM((bars, length, width), jnp.bfloat16)] * 3
            + [
                dma((3, bars)),
                pltpu.VMEM((tiles, bars, length, 2 * LANES), jnp.bfloat16),
                pltpu.VMEM((bars, tiles, rows, LANES), jnp.bfloat16),
                pltpu.VMEM((2 * R, tiles, CAP, length, 2 * LANES), jnp.bfloat16),
                [pltpu.VMEM((CAP, length, 2 * LANES), jnp.bfloat16)] * (2 * R * tiles),
                pltpu.VMEM((2, tiles, length, 2 * LANES), jnp.bfloat16),
                pltpu.VMEM((n_head, width, cols), jnp.bfloat16),
                pltpu.VMEM((n_head, tiles, bars, length, LANES), jnp.bfloat16),
                pltpu.VMEM((bars, tiles, rows, LANES), jnp.float32),
                pltpu.VMEM((bars, tiles, rows, LANES), jnp.float32),
                pltpu.VMEM((bars, tiles, rows, LANES), jnp.float32),
                dma((2 * R, tiles)),
                dma((2 * R, tiles)),
                dma((2, tiles)),
                dma((2, tiles)),
                dma((n_head - 1,)),
                dma((n_head - 1,)),
                dma,
                dma((tiles, bars // CHUNK, 3)),
                dma((tiles, bars // CHUNK, 3)),
            ],
            compiler_params=pltpu.CompilerParams(
                collective_id=0, has_side_effects=True
            ),
            name="bar_attention",
        )(key_bars, masked.reshape(bars, length), mask_qkv, *shaped, w_out)
        return out.reshape(tokens, cols)

    placed = (
        P("seq", "head"),
        P("seq", "head"),
        P("seq", "head"),
        P("seq"),
        P(None, "head"),
        P("seq", None),
        P("head", None),
    )
    return jax.shard_map(
        on_device, mesh=mesh, in_specs=placed, out_specs=P("seq", "head"), check_vma=False
    )
```

profile of v0, /device:TPU:25, one launch (start us, length us, event | category | flops | bytes accessed | tf_op | source)
XLA Modules:
  0.0 31.2 jit_solution(11255149840743504238)
XLA Ops:
  0.0 29.4 %bar_attention.1 = bf16[4,128,384]{2,1,0:T(8,128)(2,1)} custom-call(s32[4,4]{1,0:T(4,128)} %bars_hbm.1, s32[4,128]{1,0:T(4,128)} %bitcast.9, bf16[3,256]{1,0:T(4,128)(2,1)} %mask_hbm.1, bf16[4,128,256]{2,1,0:T(8,128)(2,1)} %bitcast.6, bf16[4,128,256]{2,1,0:T(8,128)(2,1)} %bitcast.7, bf16[4,128,256]{2,1,0:T(8,128)(2,1)} %bitcast.8, bf16[256,1536]{1,0:T(8,128)(2,1)} %w_ref.1), custom_call_target="tpu_custom_call" | custom-call | tf_op jit(solution)/shard_map/bar_attention/pallas_call | solution.py:335
  29.4 1.8 %copy.9 = bf16[512,384]{1,0:T(8,128)(2,1)} copy(bf16[512,384]{1,0:T(8,128)(2,1)} %bitcast.5) | data formatting | bytes 786432
where the time goes:
time: 31.4 us; the launch traced here: 31.2 us
  Pallas kernels  29.4 us (94%)
  local copies, waits for them, and re-layouts  1.78 us (6%)
    pallas_call x1, Pallas kernels, on_device(): pl.pallas_call(functools.partial(kernel, n_seq, n_head), out_shape=jax.Sh...  29.4 us
    unnamed x1, local copies, waits for them, and re-layouts  1.78 us

commit v1 on v0

v1 whole, which is shorter than its diff:
```python
import functools

import jax
import jax.numpy as jnp
from jax import lax
from jax.experimental import pallas as pl
from jax.experimental.pallas import tpu as pltpu
from jax.sharding import PartitionSpec as P

HD = 64
CAP = 2
LANES = 128
MESH = pl.DeviceIdType.MESH
NEG = -1e30


def kernel(
    n_seq, n_head, bars_hbm, masked_hbm, mask_hbm, q_hbm, k_hbm, v_hbm, w_hbm, out_hbm,
    bars, twin_bars, masked_ref, mask_ref, raw, own, give, twin, near, back, pack_own, pack_twin,
    pick_near, pick_far, q_own, q_give, q_twin, w_all, att, att_twin, part, out_ref, acc, top, tot,
    out_sem, small_sem, load_sem, w_own, bars_send, bars_recv, give_send, give_recv, q_send, q_recv,
    near_send, near_recv, back_send, back_recv, pick_send, pick_recv,
    w_send, w_recv, y_send, y_recv, att_send, att_recv,
):
    seq = lax.axis_index("seq")
    head = lax.axis_index("head")
    n_bar, bar_len, out_cols = out_ref.shape
    odd = lax.rem(seq, 2)
    other = 1 - odd
    partner = seq + 1 - 2 * odd
    outer = seq - 2 + 4 * odd
    inner = seq + 2 - 4 * odd
    has_outer = jnp.logical_and(outer >= 0, outer < n_seq)
    has_inner = jnp.logical_and(inner >= 0, inner < n_seq)
    per_tile = LANES // HD

    def slot_bar(i):
        return i + odd * (n_bar - 1 - 2 * i)

    def column(c, count):
        return c + odd * (count - 1 - 2 * c)

    def column_twin(c, count):
        return column(c, count)

    columns = bars.shape[1]

    barrier = pltpu.get_barrier_semaphore()
    peers = [lax.rem(head + step, n_head) for step in range(1, n_head)]
    count = n_head
    for there, place in ((has_outer, outer), (has_inner, inner)):
        count = count + there.astype(jnp.int32)

        @pl.when(there)
        def _(place=place):
            pl.semaphore_signal(barrier, inc=1, device_id=(place, head), device_id_type=MESH)

    pl.semaphore_signal(barrier, inc=1, device_id=(partner, head), device_id_type=MESH)
    for peer in peers:
        pl.semaphore_signal(barrier, inc=1, device_id=(seq, peer), device_id_type=MESH)

    small = [
        pltpu.make_async_copy(source, target, small_sem.at[n])
        for n, (source, target) in enumerate(
            ((masked_hbm, masked_ref), (mask_hbm, mask_ref), (bars_hbm, bars))
        )
    ]
    for load in small:
        load.start()
    loads = [
        pltpu.make_async_copy(source, raw.at[n], load_sem.at[n])
        for n, source in enumerate((k_hbm, v_hbm, q_hbm))
    ]
    for load in loads:
        load.start()
    own_w = pltpu.make_async_copy(
        w_hbm.at[:, pl.ds(pl.multiple_of(head * out_cols, LANES), out_cols)], w_all.at[head], w_own
    )
    own_w.start()

    rows = lax.broadcasted_iota(jnp.int32, (bar_len, bar_len), 0)
    cols = lax.broadcasted_iota(jnp.int32, (bar_len, bar_len), 1)
    lane = lax.broadcasted_iota(jnp.int32, (bar_len, LANES), 1)
    mine = pl.ds(pl.multiple_of(odd * LANES, LANES), LANES)
    theirs = pl.ds(pl.multiple_of(other * LANES, LANES), LANES)

    for load in small:
        load.wait()
    hits = {}

    def flag(i):
        row = masked_ref[pl.ds(slot_bar(i), 1), :]
        hits[i] = jnp.max(jnp.where(rows == cols, row, 0), axis=1, keepdims=True) == 1

    def replaced(n, i, row, tile):
        mask_row = mask_ref[row : row + 1, tile].astype(jnp.float32)
        return jnp.where(hits[i], mask_row, raw[n, slot_bar(i), :, tile].astype(jnp.float32))

    def prepare(target, i, tile):
        target[i, :, :LANES] = replaced(0, i, 1, tile).astype(jnp.bfloat16)
        target[i, :, LANES:] = replaced(1, i, 2, tile).astype(jnp.bfloat16)

    def send(source, target, send_sem, recv_sem, place):
        return pltpu.make_async_remote_copy(
            src_ref=source, dst_ref=target, send_sem=send_sem, recv_sem=recv_sem,
            device_id=place, device_id_type=MESH,
        )

    def give_copy(i):
        return send(give.at[i], twin.at[i], give_send, give_recv.at[i], (partner, head))

    give_all = send(give, twin, give_send, give_recv.at[0], (partner, head))
    q_all = send(q_give, q_twin, q_send, q_recv, (partner, head))
    near_all = send(own, near, near_send, near_recv, (outer, head))
    back_all = send(twin, back, back_send, back_recv, (inner, head))

    def near_copy(i):
        return send(own.at[i], near.at[i], near_send, near_recv, (outer, head))

    def back_copy(i):
        return send(twin.at[i], back.at[i], back_send, back_recv, (inner, head))

    def pick_copy(far):
        if far:
            return send(pack_twin, pick_far, pick_send.at[1], pick_recv.at[1], (outer, head))
        return send(pack_own, pick_near, pick_send.at[0], pick_recv.at[0], (inner, head))

    bars_copy = pltpu.make_async_remote_copy(
        src_ref=bars_hbm, dst_ref=twin_bars, send_sem=bars_send, recv_sem=bars_recv,
        device_id=(partner, head), device_id_type=MESH,
    )

    core = head + 1 - 2 * lax.rem(head, 2)
    across = lax.rem(head + 2, n_head)
    turn = lax.rem(seq // 2, 2)
    direct = across + turn * (1 - 2 * lax.rem(across, 2))
    mate = seq + 2 - 4 * turn

    def w_copy(step):
        if step == 2:
            source, target, place = w_all.at[direct], w_all.at[direct], (mate, head)
        else:
            peer = direct if step else core
            source = w_hbm.at[:, pl.ds(pl.multiple_of(peer * out_cols, LANES), out_cols)]
            target, place = w_all.at[head], (seq, peer)
        return send(source, target, w_send, w_recv.at[step], place)

    loads[0].wait()
    loads[1].wait()
    for i in range(n_bar):
        flag(i)
        prepare(give, i, theirs)
        prepare(own, i, mine)
        if i == 0:
            pl.semaphore_wait(barrier, count)
            bars_copy.start()
        give_copy(i).start()

        @pl.when(has_outer)
        def _(i=i):
            near_copy(i).start()

    for step in (1, 0):
        w_copy(step).start()

    def picks(table, c, turned):
        before = jnp.int32(0)
        chosen = [jnp.int32(0)] * CAP
        for b in range(n_bar):
            used = (table[b, c] >= 0).astype(jnp.int32)
            at = b + odd * (n_bar - 1 - 2 * b)
            if turned:
                at = n_bar - 1 - at
            for slot in range(CAP):
                chosen[slot] = chosen[slot] + jnp.where(before == slot, used * at, 0)
            before = before + used
        return chosen

    for slot, at in enumerate(picks(bars, column(columns - 1, columns), False)):
        pack_own[slot] = own[at]

    @pl.when(has_inner)
    def _():
        pick_copy(0).start()

    loads[2].wait()
    for i in range(n_bar):
        q_give[i] = (replaced(2, i, 0, theirs) * HD ** -0.5).astype(jnp.bfloat16)
    for i in range(n_bar):
        q_own[i] = (replaced(2, i, 0, mine) * HD ** -0.5).astype(jnp.bfloat16)

    @pl.when(jnp.logical_not(has_outer))
    def _():
        back[...] = jnp.zeros(back.shape, back.dtype)
        pick_near[...] = jnp.zeros(pick_near.shape, pick_near.dtype)

    @pl.when(jnp.logical_not(has_inner))
    def _():
        near[...] = jnp.zeros(near.shape, near.dtype)
        pick_far[...] = jnp.zeros(pick_far.shape, pick_far.dtype)

    for i in range(n_bar):
        give_copy(i).wait_recv()
        if i == 1:
            q_all.start()

        @pl.when(has_inner)
        def _(i=i):
            back_copy(i).start()

    bars_copy.wait_recv()
    for slot, at in enumerate(picks(twin_bars, column(0, columns), True)):
        pack_twin[slot] = twin[at]

    @pl.when(has_outer)
    def _():
        pick_copy(1).start()

    w_copy(1).wait_recv()
    w_copy(2).start()

    halves = [(lane // HD == h).astype(jnp.bfloat16) for h in range(per_tile)]

    def weigh(jobs):
        scores = []
        for query, blocks, _ in jobs:
            stacked = jnp.concatenate([query * half for half in halves], axis=0)
            row = []
            for block, usable in blocks:
                s = lax.dot_general(
                    stacked, block[:, :LANES], (((1,), (1,)), ((), ())), preferred_element_type=jnp.float32
                )
                if usable is not None:
                    s = s + jnp.where(usable, 0.0, NEG).astype(jnp.float32)
                row.append(s)
            scores.append(row)
        peaks, fades = [], []
        for row, (_, _, old) in zip(scores, jobs):
            peak = jnp.max(functools.reduce(jnp.maximum, row), axis=1, keepdims=True)
            if old is not None:
                peak = jnp.maximum(peak, top[old])
                fades.append(jnp.exp(top[old] - peak))
            else:
                fades.append(None)
            peaks.append(peak)
        totals, rounded = [], []
        for row, peak, fade, (_, _, old) in zip(scores, peaks, fades, jobs):
            raised = [jnp.exp(s - peak) for s in row]
            total = jnp.sum(functools.reduce(jnp.add, raised), axis=1, keepdims=True)
            if old is not None:
                total = total + tot[old] * fade
            totals.append(total)
            rounded.append(jnp.concatenate([r.astype(jnp.bfloat16) for r in raised], axis=1))
        sums = []
        for weight, fade, (_, blocks, old) in zip(rounded, fades, jobs):
            value = jnp.concatenate([block[:, LANES:] for block, _ in blocks], axis=0)
            weighted = jnp.dot(weight, value, preferred_element_type=jnp.float32)
            if old is not None:
                weighted = weighted + acc[old] * fade
            sums.append(weighted)
        return list(zip(peaks, totals, sums))

    def keep(slots, states):
        for slot, (peak, total, weighted) in zip(slots, states):
            top[slot] = jnp.broadcast_to(peak, top.shape[1:])
            tot[slot] = jnp.broadcast_to(total, tot.shape[1:])
            acc[slot] = weighted

    def finish(state):
        _, total, weighted = state
        done = weighted / total
        result = done[:bar_len]
        for h in range(1, per_tile):
            result = jnp.where(lane // HD == h, done[h * bar_len : (h + 1) * bar_len], result)
        return result.astype(jnp.bfloat16)

    def whole(table, b, c, ref, turned):
        wanted = table[b, c]
        at = lax.rem(jnp.maximum(wanted, 0), n_bar)
        at = at + odd * (n_bar - 1 - 2 * at)
        if turned:
            at = n_bar - 1 - at
        return ref[at], wanted >= 0

    def picked(table, b, c, ref):
        wanted = table[b, c]
        slot = jnp.int32(0)
        for o in range(n_bar):
            held = table[o, c]
            slot = slot + jnp.logical_and(held >= 0, held < wanted).astype(jnp.int32)
        return ref[jnp.minimum(slot, CAP - 1)], wanted >= 0

    def att_copy(order, i, kind):
        tile = odd + order * (1 - 2 * odd)
        slot = across if kind == 2 else head
        piece = att.at[slot, tile] if i is None else att.at[slot, tile, i]
        recv = att_recv.at[order, i if kind == 1 else n_bar + kind // 2]
        return pltpu.make_async_remote_copy(
            src_ref=piece, dst_ref=piece, send_sem=att_send, recv_sem=recv,
            device_id=(seq, across if kind == 1 else core), device_id_type=MESH,
        )

    def y_copy(i):
        return send(att_twin.at[i], att.at[head, odd, i], y_send, y_recv.at[i], (partner, head))

    def relay(order, i):
        att_copy(order, i, 1).wait_recv()
        att_copy(order, i, 2).start()

    @pl.when(has_outer)
    def _():
        pick_copy(0).wait_recv()

    @pl.when(has_inner)
    def _():
        near_all.wait_recv()

    last = n_bar - 1

    def band(mirror, i, beyond):
        blocks = [(mirror[n], None) for n in range(max(i - 1, 0), min(i + 2, n_bar))]
        if i == last:
            blocks.append((beyond[last], None))
        return blocks

    def own_first(i):
        b = slot_bar(i)
        blocks = band(own, i, twin)
        blocks.append(picked(bars, b, column(0, columns), pick_near))
        blocks.append(whole(bars, b, column(2, columns), twin, True))
        blocks.append(whole(bars, b, column(3, columns), near, False))
        return q_own[i], blocks, None

    def own_rest(i):
        blocks = [whole(bars, slot_bar(i), column(1, columns), back, True)]
        if i == 0:
            blocks.append((back[0], has_outer))
        return q_own[i], blocks, i

    def twin_bar(i):
        return last - i + odd * (2 * i - last)

    def twin_first(i):
        b = twin_bar(i)
        blocks = band(twin, i, own)
        if i == 0:
            blocks.append((near[0], has_inner))
        blocks.append(whole(twin_bars, b, column(0, columns), back, True))
        blocks.append(whole(twin_bars, b, column(1, columns), own, False))
        blocks.append(whole(twin_bars, b, column(2, columns), near, False))
        return q_twin[i], blocks, None

    def twin_rest(i):
        return q_twin[i], [picked(twin_bars, twin_bar(i), column(3, columns), pick_far)], n_bar + i

    slots = range(n_bar)
    keep(slots, weigh([own_first(i) for i in slots]))

    @pl.when(has_outer)
    def _():
        back_all.wait_recv()

    for i, state in zip(slots, weigh([own_rest(i) for i in slots])):
        att[head, odd, i] = finish(state)
    for i in slots:
        att_copy(0, i, 1).start()
        att_copy(0, i, 0).start()

    q_all.wait_recv()
    keep([n_bar + i for i in slots], weigh([twin_first(i) for i in slots]))

    @pl.when(has_inner)
    def _():
        pick_copy(1).wait_recv()

    for i, state in zip(slots, weigh([twin_rest(i) for i in slots])):
        att_twin[i] = finish(state)
    for i in slots:
        y_copy(i).start()

    def pass_on(i):
        y_copy(i).wait_recv()
        att_copy(1, i, 1).start()
        att_copy(1, i, 0).start()

    for i in range(last):
        relay(0, i)
    pass_on(0)
    relay(0, last)
    for i in range(1, n_bar):
        pass_on(i)

    own_w.wait()
    w_copy(0).wait_recv()
    w_copy(2).wait_recv()
    att_copy(0, None, 0).wait_recv()
    att_copy(0, None, 2).wait_recv()

    def out_copy(i):
        return pltpu.make_async_copy(out_ref.at[i], out_hbm.at[slot_bar(i)], out_sem)

    def project(tile, i):
        lhs = jnp.concatenate([att[m, tile, i] for m in range(n_head)], axis=1)
        at = pl.ds(pl.multiple_of(tile * LANES, LANES), LANES)
        rhs = jnp.concatenate([w_all[m, at, :] for m in range(n_head)], axis=0)
        return jnp.dot(lhs, rhs, preferred_element_type=jnp.float32)

    for i in range(n_bar):
        part[i] = project(odd, i)
        relay(1, i)
    att_copy(1, None, 0).wait_recv()
    att_copy(1, None, 2).wait_recv()
    for i in slots:
        out_ref[i] = (part[i] + project(other, i)).astype(jnp.bfloat16)
        out_copy(i).start()

    pltpu.make_async_copy(out_ref, out_hbm, out_sem).wait()
    bars_copy.wait_send()
    give_all.wait_send()
    q_all.wait_send()
    send(att_twin, att.at[head, odd], y_send, y_recv.at[0], (partner, head)).wait_send()
    for half in (att.at[0 : n_head - 1],):
        send(half, half, att_send, att_recv.at[0, 0], (seq, core)).wait_send()
    blocks = w_all.at[0:3]
    send(blocks, blocks, w_send, w_recv.at[0], (seq, core)).wait_send()

    @pl.when(has_outer)
    def _():
        near_all.wait_send()
        pick_copy(1).wait_send()

    @pl.when(has_inner)
    def _():
        back_all.wait_send()
        pick_copy(0).wait_send()


def solution(mesh):
    n_seq, n_head = mesh.shape["seq"], mesh.shape["head"]

    def on_device(queries, keys, values, masked, mask_qkv, key_bars, w_out):
        tokens, width = queries.shape
        bars, slots = key_bars.shape
        length = tokens // bars
        cols = w_out.shape[1] // n_head
        tiles = width // LANES
        shaped = [x.reshape(bars, length, width) for x in (queries, keys, values)]
        hbm = pl.BlockSpec(memory_space=pltpu.HBM)
        dma = pltpu.SemaphoreType.DMA
        bf16 = jnp.bfloat16
        pair = (bars, length, 2 * LANES)
        single = (bars, length, LANES)
        some = (CAP, length, 2 * LANES)
        out = pl.pallas_call(
            functools.partial(kernel, n_seq, n_head),
            out_shape=jax.ShapeDtypeStruct((bars, length, cols), bf16),
            in_specs=[hbm] * 7,
            out_specs=hbm,
            scratch_shapes=[
                pltpu.SMEM(key_bars.shape, jnp.int32),
                pltpu.SMEM(key_bars.shape, jnp.int32),
                pltpu.VMEM((bars, length), jnp.int32),
                pltpu.VMEM(mask_qkv.shape, bf16),
                pltpu.VMEM((3, bars, length, width), bf16),
            ]
            + [pltpu.VMEM(pair, bf16)] * 5
            + [pltpu.VMEM(some, bf16)] * 4
            + [pltpu.VMEM(single, bf16)] * 3
            + [
                pltpu.VMEM((n_head, width, cols), bf16),
                pltpu.VMEM((n_head, tiles, bars, length, LANES), bf16),
                pltpu.VMEM(single, bf16),
                pltpu.VMEM((bars, length, cols), jnp.float32),
                pltpu.VMEM((bars, length, cols), bf16),
            ]
            + [pltpu.VMEM((2 * bars, LANES // HD * length, LANES), jnp.float32)] * 3
            + [
                dma,
                dma((3,)),
                dma((3,)),
                dma,
                dma,
                dma,
                dma,
                dma((bars,)),
                dma,
                dma,
                dma,
                dma,
                dma,
                dma,
                dma((2,)),
                dma((2,)),
                dma,
                dma((3,)),
                dma,
                dma((bars,)),
                dma,
                dma((2, bars + 2)),
            ],
            compiler_params=pltpu.CompilerParams(
                collective_id=0, has_side_effects=True
            ),
            name="bar_attention",
        )(key_bars, masked.reshape(bars, length), mask_qkv, *shaped, w_out)
        return out.reshape(tokens, cols)

    placed = (
        P("seq", "head"),
        P("seq", "head"),
        P("seq", "head"),
        P("seq"),
        P(None, "head"),
        P("seq", None),
        P("head", None),
    )
    return jax.shard_map(
        on_device, mesh=mesh, in_specs=placed, out_specs=P("seq", "head"), check_vma=False
    )
```

time: 31.4 us -> 30.1 us (0.959)
  the two profiles are of different devices: /device:TPU:25 before, /device:TPU:1 now
where the time goes in v1:
time: 30.1 us; the launch traced here: 29.9 us
  Pallas kernels  28.1 us (93%)
  local copies, waits for them, and re-layouts  1.78 us (6%)
    pallas_call x1, Pallas kernels, on_device(): pl.pallas_call(functools.partial(kernel, n_seq, n_head), out_shape=jax.Sh...  28.1 us
    unnamed x1, local copies, waits for them, and re-layouts  1.78 us

profile of v1, /device:TPU:1, one launch (start us, length us, event | category | flops | bytes accessed | tf_op | source)
XLA Modules:
  0.0 29.9 jit_solution(5579041017598532056)
XLA Ops:
  0.0 28.1 %bar_attention.1 = bf16[4,128,384]{2,1,0:T(8,128)(2,1)} custom-call(s32[4,4]{1,0:T(4,128)} %bars_hbm.1, s32[4,128]{1,0:T(4,128)} %bitcast.9, bf16[3,256]{1,0:T(4,128)(2,1)} %mask_hbm.1, bf16[4,128,256]{2,1,0:T(8,128)(2,1)} %bitcast.6, bf16[4,128,256]{2,1,0:T(8,128)(2,1)} %bitcast.7, bf16[4,128,256]{2,1,0:T(8,128)(2,1)} %bitcast.8, bf16[256,1536]{1,0:T(8,128)(2,1)} %w_hbm.1), custom_call_target="tpu_custom_call" | custom-call | tf_op jit(solution)/shard_map/bar_attention/pallas_call | solution.py:454
  28.1 1.8 %copy.9 = bf16[512,384]{1,0:T(8,128)(2,1)} copy(bf16[512,384]{1,0:T(8,128)(2,1)} %bitcast.5) | data formatting | bytes 786432

commit v2 on v1

--- a/solution.py
+++ b/solution.py
@@ -15,12 +15,12 @@
 
 
 def kernel(
-    n_seq, n_head, bars_hbm, masked_hbm, mask_hbm, q_hbm, k_hbm, v_hbm, w_hbm, out_hbm,
+    n_seq, n_head, bars_hbm, masked_hbm, mask_hbm, q_hbm, k_hbm, v_hbm, w_hbm, out_ref,
     bars, twin_bars, masked_ref, mask_ref, raw, own, give, twin, near, back, pack_own, pack_twin,
-    pick_near, pick_far, q_own, q_give, q_twin, w_all, att, att_twin, part, out_ref, acc, top, tot,
-    out_sem, small_sem, load_sem, w_own, bars_send, bars_recv, give_send, give_recv, q_send, q_recv,
+    pick_near, pick_far, q_own, q_give, q_twin, w_all, att, att_twin, part, acc, top, tot,
+    small_sem, load_sem, w_own, bars_send, bars_recv, give_send, give_recv, q_send, q_recv,
     near_send, near_recv, back_send, back_recv, pick_send, pick_recv,
-    w_send, w_recv, y_send, y_recv, att_send, att_recv,
+    w_send, w_recv, y_send, y_recv, att_send, att_recv, late_recv,
 ):
     seq = lax.axis_index("seq")
     head = lax.axis_index("head")
@@ -47,7 +47,8 @@
 
     barrier = pltpu.get_barrier_semaphore()
     peers = [lax.rem(head + step, n_head) for step in range(1, n_head)]
-    count = n_head
+    across = lax.rem(head + 2, n_head)
+    count = n_head + 1
     for there, place in ((has_outer, outer), (has_inner, inner)):
         count = count + there.astype(jnp.int32)
 
@@ -55,7 +56,8 @@
         def _(place=place):
             pl.semaphore_signal(barrier, inc=1, device_id=(place, head), device_id_type=MESH)
 
-    pl.semaphore_signal(barrier, inc=1, device_id=(partner, head), device_id_type=MESH)
+    for place in (head, across):
+        pl.semaphore_signal(barrier, inc=1, device_id=(partner, place), device_id_type=MESH)
     for peer in peers:
         pl.semaphore_signal(barrier, inc=1, device_id=(seq, peer), device_id_type=MESH)
 
@@ -131,7 +133,6 @@
     )
 
     core = head + 1 - 2 * lax.rem(head, 2)
-    across = lax.rem(head + 2, n_head)
     turn = lax.rem(seq // 2, 2)
     direct = across + turn * (1 - 2 * lax.rem(across, 2))
     mate = seq + 2 - 4 * turn
@@ -215,9 +216,6 @@
     @pl.when(has_outer)
     def _():
         pick_copy(1).start()
-
-    w_copy(1).wait_recv()
-    w_copy(2).start()
 
     halves = [(lane // HD == h).astype(jnp.bfloat16) for h in range(per_tile)]
 
@@ -294,7 +292,10 @@
         tile = odd + order * (1 - 2 * odd)
         slot = across if kind == 2 else head
         piece = att.at[slot, tile] if i is None else att.at[slot, tile, i]
-        recv = att_recv.at[order, i if kind == 1 else n_bar + kind // 2]
+        if order and kind != 1:
+            recv = late_recv.at[i, kind // 2]
+        else:
+            recv = att_recv.at[order, i if kind == 1 else n_bar + kind // 2]
         return pltpu.make_async_remote_copy(
             src_ref=piece, dst_ref=piece, send_sem=att_send, recv_sem=recv,
             device_id=(seq, across if kind == 1 else core), device_id_type=MESH,
@@ -302,6 +303,9 @@
 
     def y_copy(i):
         return send(att_twin.at[i], att.at[head, odd, i], y_send, y_recv.at[i], (partner, head))
+
+    def corner_copy(i):
+        return send(att_twin.at[i], att.at[head, odd, i], att_send, att_recv.at[1, i], (partner, across))
 
     def relay(order, i):
         att_copy(order, i, 1).wait_recv()
@@ -345,16 +349,21 @@
         blocks = band(twin, i, own)
         if i == 0:
             blocks.append((near[0], has_inner))
-        blocks.append(whole(twin_bars, b, column(0, columns), back, True))
         blocks.append(whole(twin_bars, b, column(1, columns), own, False))
         blocks.append(whole(twin_bars, b, column(2, columns), near, False))
         return q_twin[i], blocks, None
 
     def twin_rest(i):
-        return q_twin[i], [picked(twin_bars, twin_bar(i), column(3, columns), pick_far)], n_bar + i
+        b = twin_bar(i)
+        blocks = [whole(twin_bars, b, column(0, columns), back, True)]
+        blocks.append(picked(twin_bars, b, column(3, columns), pick_far))
+        return q_twin[i], blocks, n_bar + i
 
     slots = range(n_bar)
     keep(slots, weigh([own_first(i) for i in slots]))
+
+    q_all.wait_recv()
+    keep([n_bar + i for i in slots], weigh([twin_first(i) for i in slots]))
 
     @pl.when(has_outer)
     def _():
@@ -365,9 +374,8 @@
     for i in slots:
         att_copy(0, i, 1).start()
         att_copy(0, i, 0).start()
-
-    q_all.wait_recv()
-    keep([n_bar + i for i in slots], weigh([twin_first(i) for i in slots]))
+    w_copy(1).wait_recv()
+    w_copy(2).start()
 
     @pl.when(has_inner)
     def _():
@@ -376,19 +384,14 @@
     for i, state in zip(slots, weigh([twin_rest(i) for i in slots])):
         att_twin[i] = finish(state)
     for i in slots:
+        corner_copy(i).start()
         y_copy(i).start()
-
-    def pass_on(i):
+    for i in slots:
+        relay(0, i)
+    for i in slots:
         y_copy(i).wait_recv()
-        att_copy(1, i, 1).start()
         att_copy(1, i, 0).start()
-
-    for i in range(last):
-        relay(0, i)
-    pass_on(0)
-    relay(0, last)
-    for i in range(1, n_bar):
-        pass_on(i)
+        relay(1, i)
 
     own_w.wait()
     w_copy(0).wait_recv()
@@ -396,31 +399,30 @@
     att_copy(0, None, 0).wait_recv()
     att_copy(0, None, 2).wait_recv()
 
-    def out_copy(i):
-        return pltpu.make_async_copy(out_ref.at[i], out_hbm.at[slot_bar(i)], out_sem)
-
-    def project(tile, i):
-        lhs = jnp.concatenate([att[m, tile, i] for m in range(n_head)], axis=1)
+    def project(members, tile, lhs_of):
+        lhs = jnp.concatenate([lhs_of(m, tile) for m in members], axis=1)
         at = pl.ds(pl.multiple_of(tile * LANES, LANES), LANES)
-        rhs = jnp.concatenate([w_all[m, at, :] for m in range(n_head)], axis=0)
+        rhs = jnp.concatenate([w_all[m, at, :] for m in members], axis=0)
         return jnp.dot(lhs, rhs, preferred_element_type=jnp.float32)
 
-    for i in range(n_bar):
-        part[i] = project(odd, i)
-        relay(1, i)
-    att_copy(1, None, 0).wait_recv()
-    att_copy(1, None, 2).wait_recv()
+    def all_bars(m, tile):
+        return att[m, tile].reshape(n_bar * bar_len, LANES)
+
+    beside = across + 1 - 2 * lax.rem(across, 2)
+    part[...] = project(range(n_head), odd, all_bars)
+    part[...] += project((head, across), other, all_bars)
     for i in slots:
-        out_ref[i] = (part[i] + project(other, i)).astype(jnp.bfloat16)
-        out_copy(i).start()
-
-    pltpu.make_async_copy(out_ref, out_hbm, out_sem).wait()
+        att_copy(1, i, 0).wait_recv()
+        att_copy(1, i, 2).wait_recv()
+        rest = project((core, beside), other, lambda m, tile: att[m, tile, i])
+        out_ref[slot_bar(i)] = (part[i * bar_len : (i + 1) * bar_len] + rest).astype(jnp.bfloat16)
+
     bars_copy.wait_send()
     give_all.wait_send()
     q_all.wait_send()
     send(att_twin, att.at[head, odd], y_send, y_recv.at[0], (partner, head)).wait_send()
-    for half in (att.at[0 : n_head - 1],):
-        send(half, half, att_send, att_recv.at[0, 0], (seq, core)).wait_send()
+    sent = att.at[0 : n_head - 1]
+    send(sent, sent, att_send, att_recv.at[0, 0], (seq, core)).wait_send()
     blocks = w_all.at[0:3]
     send(blocks, blocks, w_send, w_recv.at[0], (seq, core)).wait_send()
 
@@ -453,9 +455,9 @@
         some = (CAP, length, 2 * LANES)
         out = pl.pallas_call(
             functools.partial(kernel, n_seq, n_head),
-            out_shape=jax.ShapeDtypeStruct((bars, length, cols), bf16),
+            out_shape=pltpu.VMEM((bars, length, cols), bf16),
             in_specs=[hbm] * 7,
-            out_specs=hbm,
+            out_specs=pl.BlockSpec(memory_space=pltpu.VMEM),
             scratch_shapes=[
                 pltpu.SMEM(key_bars.shape, jnp.int32),
                 pltpu.SMEM(key_bars.shape, jnp.int32),
@@ -470,12 +472,10 @@
                 pltpu.VMEM((n_head, width, cols), bf16),
                 pltpu.VMEM((n_head, tiles, bars, length, LANES), bf16),
                 pltpu.VMEM(single, bf16),
-                pltpu.VMEM((bars, length, cols), jnp.float32),
-                pltpu.VMEM((bars, length, cols), bf16),
+                pltpu.VMEM((tokens, cols), jnp.float32),
             ]
             + [pltpu.VMEM((2 * bars, LANES // HD * length, LANES), jnp.float32)] * 3
             + [
-                dma,
                 dma((3,)),
                 dma((3,)),
                 dma,
@@ -497,12 +497,13 @@
                 dma((bars,)),
                 dma,
                 dma((2, bars + 2)),
+                dma((bars, 2)),
             ],
             compiler_params=pltpu.CompilerParams(
-                collective_id=0, has_side_effects=True
+                collective_id=0, has_side_effects=True, vmem_limit_bytes=40 * 1024 * 1024
             ),
             name="bar_attention",
-        )(key_bars, masked.reshape(bars, length), mask_qkv, *shaped, w_out)
+        )(*(pltpu.with_memory_space_constraint(x, pltpu.HBM) for x in (key_bars, masked.reshape(bars, length), mask_qkv, *shaped, w_out)))
         return out.reshape(tokens, cols)
 
     placed = (

time: 30.1 us -> 25.7 us (0.85)
  the two profiles are of different devices: /device:TPU:1 before, /device:TPU:0 now
where the time goes in v2:
time: 25.7 us; the launch traced here: 25.6 us
  Pallas kernels  24.8 us (96%)
  local copies, waits for them, and re-layouts  0.75 us (3%)
    pallas_call x1, Pallas kernels, on_device(): pl.pallas_call(functools.partial(kernel, n_seq, n_head), out_shape=pltpu....  24.8 us
    unnamed x1, local copies, waits for them, and re-layouts  0.75 us

profile of v2, /device:TPU:0, one launch (start us, length us, event | category | flops | bytes accessed | tf_op | source)
XLA Modules:
  0.0 25.6 jit_solution(6840885243205101868)
XLA Ops:
  0.0 24.8 %bar_attention.1 = bf16[4,128,384]{2,1,0:T(8,128)(2,1)S(1)} custom-call(s32[4,4]{1,0:T(4,128)} %bars_hbm.1, s32[4,128]{1,0:T(4,128)} %bitcast.9, bf16[3,256]{1,0:T(4,128)(2,1)} %mask_hbm.1, bf16[4,128,256]{2,1,0:T(8,128)(2,1)} %bitcast.6, bf16[4,128,256]{2,1,0:T(8,128)(2,1)} %bitcast.7, bf16[4,128,256]{2,1,0:T(8,128)(2,1)} %bitcast.8, bf16[256,1536]{1,0:T(8,128)(2,1)} %w_hbm.1), custom_call_target="tpu_custom_call" | custom-call | tf_op jit(solution)/shard_map/bar_attention/pallas_call | solution.py:456
  24.8 0.7 %copy.9 = bf16[512,384]{1,0:T(8,128)(2,1)} copy(bf16[512,384]{1,0:T(8,128)(2,1)S(1)} %bitcast.5) | data formatting | bytes 786432

commit v3 on v2

--- a/solution.py
+++ b/solution.py
@@ -9,6 +9,7 @@
 
 HD = 64
 CAP = 2
+GROUP = 2
 LANES = 128
 MESH = pl.DeviceIdType.MESH
 NEG = -1e30
@@ -369,13 +370,14 @@
     def _():
         back_all.wait_recv()
 
-    for i, state in zip(slots, weigh([own_rest(i) for i in slots])):
-        att[head, odd, i] = finish(state)
-    for i in slots:
-        att_copy(0, i, 1).start()
-        att_copy(0, i, 0).start()
-    w_copy(1).wait_recv()
-    w_copy(2).start()
+    def finish_own():
+        for i, state in zip(slots, weigh([own_rest(i) for i in slots])):
+            att[head, odd, i] = finish(state)
+        for i in slots:
+            att_copy(0, i, 1).start()
+            att_copy(0, i, 0).start()
+
+    pl.when(odd == 0)(finish_own)
 
     @pl.when(has_inner)
     def _():
@@ -386,36 +388,47 @@
     for i in slots:
         corner_copy(i).start()
         y_copy(i).start()
+
+    pl.when(odd == 1)(finish_own)
+    w_copy(1).wait_recv()
+    w_copy(2).start()
+
     for i in slots:
         relay(0, i)
-    for i in slots:
+    def project(members, tile, span):
+        lhs = jnp.concatenate([att[m, tile, span].reshape(-1, LANES) for m in members], axis=1)
+        at = pl.ds(pl.multiple_of(tile * LANES, LANES), LANES)
+        rhs = jnp.concatenate([w_all[m, at, :] for m in members], axis=0)
+        return jnp.dot(lhs, rhs, preferred_element_type=jnp.float32)
+
+    def forward(i):
         y_copy(i).wait_recv()
         att_copy(1, i, 0).start()
         relay(1, i)
 
+    near_side, far_side = (head, across), (core, across + 1 - 2 * lax.rem(across, 2))
+    every = slice(0, n_bar)
+    for i in slots[: n_bar // 2]:
+        forward(i)
     own_w.wait()
     w_copy(0).wait_recv()
     w_copy(2).wait_recv()
+    part[...] = project(near_side, odd, every)
+    for i in slots[n_bar // 2 :]:
+        forward(i)
+    part[...] += project(near_side, other, every)
     att_copy(0, None, 0).wait_recv()
     att_copy(0, None, 2).wait_recv()
-
-    def project(members, tile, lhs_of):
-        lhs = jnp.concatenate([lhs_of(m, tile) for m in members], axis=1)
-        at = pl.ds(pl.multiple_of(tile * LANES, LANES), LANES)
-        rhs = jnp.concatenate([w_all[m, at, :] for m in members], axis=0)
-        return jnp.dot(lhs, rhs, preferred_element_type=jnp.float32)
-
-    def all_bars(m, tile):
-        return att[m, tile].reshape(n_bar * bar_len, LANES)
-
-    beside = across + 1 - 2 * lax.rem(across, 2)
-    part[...] = project(range(n_head), odd, all_bars)
-    part[...] += project((head, across), other, all_bars)
-    for i in slots:
-        att_copy(1, i, 0).wait_recv()
-        att_copy(1, i, 2).wait_recv()
-        rest = project((core, beside), other, lambda m, tile: att[m, tile, i])
-        out_ref[slot_bar(i)] = (part[i * bar_len : (i + 1) * bar_len] + rest).astype(jnp.bfloat16)
+    part[...] += project(far_side, odd, every)
+    for g in range(0, n_bar, GROUP):
+        for i in slots[g : g + GROUP]:
+            att_copy(1, i, 0).wait_recv()
+            att_copy(1, i, 2).wait_recv()
+        rest = project(far_side, other, slice(g, g + GROUP))
+        for i in slots[g : g + GROUP]:
+            row = (i - g) * bar_len
+            whole_bar = part[i * bar_len : (i + 1) * bar_len] + rest[row : row + bar_len]
+            out_ref[slot_bar(i)] = whole_bar.astype(jnp.bfloat16)
 
     bars_copy.wait_send()
     give_all.wait_send()

time: 25.7 us -> 25.4 us (0.988)
  the two profiles are of different devices: /device:TPU:0 before, /device:TPU:1 now
where the time goes in v3:
time: 25.4 us; the launch traced here: 25.3 us
  Pallas kernels  24.5 us (96%)
  local copies, waits for them, and re-layouts  0.75 us (3%)
    pallas_call x1, Pallas kernels, on_device(): pl.pallas_call(functools.partial(kernel, n_seq, n_head), out_shape=pltpu....  24.5 us
    unnamed x1, local copies, waits for them, and re-layouts  0.75 us

profile of v3, /device:TPU:1, one launch (start us, length us, event | category | flops | bytes accessed | tf_op | source)
XLA Modules:
  0.0 25.3 jit_solution(17409513950167514060)
XLA Ops:
  0.0 24.5 %bar_attention.1 = bf16[4,128,384]{2,1,0:T(8,128)(2,1)S(1)} custom-call(s32[4,4]{1,0:T(4,128)} %bars_hbm.1, s32[4,128]{1,0:T(4,128)} %bitcast.9, bf16[3,256]{1,0:T(4,128)(2,1)} %mask_hbm.1, bf16[4,128,256]{2,1,0:T(8,128)(2,1)} %bitcast.6, bf16[4,128,256]{2,1,0:T(8,128)(2,1)} %bitcast.7, bf16[4,128,256]{2,1,0:T(8,128)(2,1)} %bitcast.8, bf16[256,1536]{1,0:T(8,128)(2,1)} %w_hbm.1), custom_call_target="tpu_custom_call" | custom-call | tf_op jit(solution)/shard_map/bar_attention/pallas_call | solution.py:469
  24.5 0.7 %copy.9 = bf16[512,384]{1,0:T(8,128)(2,1)} copy(bf16[512,384]{1,0:T(8,128)(2,1)S(1)} %bitcast.5) | data formatting | bytes 786432

commit v4 on v3

--- a/solution.py
+++ b/solution.py
@@ -393,8 +393,6 @@
     w_copy(1).wait_recv()
     w_copy(2).start()
 
-    for i in slots:
-        relay(0, i)
     def project(members, tile, span):
         lhs = jnp.concatenate([att[m, tile, span].reshape(-1, LANES) for m in members], axis=1)
         at = pl.ds(pl.multiple_of(tile * LANES, LANES), LANES)
@@ -409,7 +407,11 @@
     near_side, far_side = (head, across), (core, across + 1 - 2 * lax.rem(across, 2))
     every = slice(0, n_bar)
     for i in slots[: n_bar // 2]:
+        relay(0, i)
+    for i in slots[: n_bar // 2]:
         forward(i)
+    for i in slots[n_bar // 2 :]:
+        relay(0, i)
     own_w.wait()
     w_copy(0).wait_recv()
     w_copy(2).wait_recv()

time: 25.4 us -> 25.4 us (level)
  no operation moved by 1% of the time
where the time goes in v4:
time: 25.4 us; the launch traced here: 25.3 us
  Pallas kernels  24.5 us (96%)
  local copies, waits for them, and re-layouts  0.75 us (3%)
    pallas_call x1, Pallas kernels, on_device(): pl.pallas_call(functools.partial(kernel, n_seq, n_head), out_shape=pltpu....  24.5 us
    unnamed x1, local copies, waits for them, and re-layouts  0.75 us

profile of v4, /device:TPU:1, one launch (start us, length us, event | category | flops | bytes accessed | tf_op | source)
XLA Modules:
  0.0 25.3 jit_solution(16340581769012987336)
XLA Ops:
  0.0 24.5 %bar_attention.1 = bf16[4,128,384]{2,1,0:T(8,128)(2,1)S(1)} custom-call(s32[4,4]{1,0:T(4,128)} %bars_hbm.1, s32[4,128]{1,0:T(4,128)} %bitcast.9, bf16[3,256]{1,0:T(4,128)(2,1)} %mask_hbm.1, bf16[4,128,256]{2,1,0:T(8,128)(2,1)} %bitcast.6, bf16[4,128,256]{2,1,0:T(8,128)(2,1)} %bitcast.7, bf16[4,128,256]{2,1,0:T(8,128)(2,1)} %bitcast.8, bf16[256,1536]{1,0:T(8,128)(2,1)} %w_hbm.1), custom_call_target="tpu_custom_call" | custom-call | tf_op jit(solution)/shard_map/bar_attention/pallas_call | solution.py:471
  24.5 0.7 %copy.9 = bf16[512,384]{1,0:T(8,128)(2,1)} copy(bf16[512,384]{1,0:T(8,128)(2,1)S(1)} %bitcast.5) | data formatting | bytes 786432
